TPU v7x, 256 devices: a whole 4x4x8 slice. The times are simulated.
256 devices in a mesh: row: 16 (over x, z_lo), col: 16 (over y, z_hi, core).
Axes of the slice: x: 4, y: 4, z: 8 (z_hi: 2, z_lo: 4; z = z_hi * 4 + z_lo), core: 2. Of those that a mesh axis runs over, the one named last changes fastest.
Arguments:
- potential: float32 [32, 64, 512], P('row', 'col'), may hold values from -6 to 6
- basis: bfloat16 [32, 64, 384, 512], P('row', 'col'), may hold values from -6 to 6
- hamiltonian: bfloat16 [6144, 6144], P('row', 'col'), may hold values from -0.078125 to 0.078125
- density: bfloat16 [2, 6144, 6144], P(None, 'row', 'col'), may hold values from -6 to 6
- hmask: int32 [48, 48], replicated, may hold values from 0 to 1, as said below
- pmask: int32 [48, 48], replicated, may hold values from 0 to 1, as said below
Outputs:
- propagated: bfloat16 [2, 6144, 6144], P(None, 'row', 'col')
Inputs may be any that keep to these rules, and one draw needn't show every extreme that they name: hmask[I, I] is always 1; every other block is 1 with probability 1/2, independently. pmask follows the same law as hmask, drawn independently.
All inputs are finite; a program needn't handle non-finite values.
Results may differ from a plain program's by a relative error of at most 0.0062.
Values may be sent and summed in bfloat16 or wider, within the bound.
A program may use at most 64 MiB of HBM per device.

v0:
```python
import jax
import jax.numpy as jnp
from jax import lax
from jax.sharding import PartitionSpec as P

BLK = 128
KAPPA = 0.4
TIME_STEP = 0.5


def extended_2(block, sides, width):
    for axis, dim in sides:
        count = lax.axis_size(axis)
        forward = [(i, i + 1) for i in range(count - 1)]
        backward = [(target, source) for source, target in forward]
        low = lax.ppermute(
            lax.slice_in_dim(block, block.shape[dim] - width, None, axis=dim), axis, forward
        )
        high = lax.ppermute(lax.slice_in_dim(block, 0, width, axis=dim), axis, backward)
        block = jnp.concatenate([low, block, high], axis=dim)
    return block


def shards(potential, basis, hamiltonian, density, hmask, pmask):
    width_x, width_y, depth_z = potential.shape
    extended = extended_2(potential, (("row", 0), ("col", 1)), 1)
    padded = jnp.pad(extended, ((0, 0), (0, 0), (1, 1)))
    beside = padded[2:, 1:-1, 1:-1] + padded[:-2, 1:-1, 1:-1]
    beside = beside + padded[1:-1, 2:, 1:-1] + padded[1:-1, :-2, 1:-1]
    beside = beside + padded[1:-1, 1:-1, 2:] + padded[1:-1, 1:-1, :-2]
    effective = potential + KAPPA * (beside - 6.0 * potential)
    blocks_here = basis.shape[2] // BLK
    weighted = (basis * effective[:, :, None, :]).astype(jnp.bfloat16)
    partial_blocks = jnp.einsum(
        "xykaz,xykbz->kab",
        weighted.reshape(width_x, width_y, blocks_here, BLK, depth_z),
        basis.reshape(width_x, width_y, blocks_here, BLK, depth_z),
        preferred_element_type=jnp.float32,
    )
    summed = lax.psum(partial_blocks, "col")
    factor = float(BLK * width_x * width_y * depth_z * lax.axis_size("col")) ** (-0.5)
    potential_blocks = (summed * factor).astype(jnp.bfloat16)
    block_total = hmask.shape[0]
    blocks_wide = block_total // lax.axis_size("col")
    row_start = lax.axis_index("row") * blocks_here
    col_start = lax.axis_index("col") * blocks_wide
    hpattern = lax.dynamic_slice(hmask, (row_start, col_start), (blocks_here, blocks_wide))
    ppattern = lax.dynamic_slice(pmask, (row_start, col_start), (blocks_here, blocks_wide))
    masked_h = (
        hamiltonian.reshape(blocks_here, BLK, blocks_wide, BLK)
        * hpattern[:, None, :, None].astype(jnp.bfloat16)
    ).reshape(blocks_here * BLK, blocks_wide * BLK)
    masked_p = (
        density.reshape(2, blocks_here, BLK, blocks_wide, BLK)
        * ppattern[None, :, None, :, None].astype(jnp.bfloat16)
    ).reshape(2, blocks_here * BLK, blocks_wide * BLK)

    def diagonal_term(operand):
        local = jnp.einsum(
            "kab,skbc->skac",
            potential_blocks,
            operand.reshape(2, blocks_here, BLK, operand.shape[2]),
            preferred_element_type=jnp.float32,
        )
        return local.reshape(2, blocks_here * BLK, operand.shape[2])

    def apply(operand):
        column_whole = lax.all_gather(operand, "row", axis=1, tiled=True)
        remote = jnp.einsum(
            "rk,skc->src",
            lax.all_gather(masked_h, "col", axis=1, tiled=True),
            column_whole,
            preferred_element_type=jnp.float32,
        )
        return remote + diagonal_term(operand)

    first = apply(masked_p)
    first_rounded = first.astype(jnp.bfloat16)
    second = apply(first_rounded)
    base = masked_p.astype(jnp.float32)
    half_square = 0.5 * TIME_STEP * TIME_STEP
    real_part = base[0] + TIME_STEP * first[1] - half_square * second[0]
    imag_part = base[1] - TIME_STEP * first[0] - half_square * second[1]
    stacked = jnp.stack([real_part, imag_part]).reshape(2, blocks_here, BLK, blocks_wide, BLK)
    stacked = stacked * ppattern[None, :, None, :, None].astype(jnp.float32)
    return stacked.reshape(2, blocks_here * BLK, blocks_wide * BLK).astype(jnp.bfloat16)


def solution(mesh):
    in_specs = (
        P("row", "col", None),
        P("row", "col", None, None),
        P("row", "col"),
        P(None, "row", "col"),
        P(),
        P(),
    )
    out_specs = P(None, "row", "col")
    return jax.shard_map(shards, mesh=mesh, in_specs=in_specs, out_specs=out_specs, check_vma=False)
```

profile of v0, /device:TPU:1, one launch (start us, length us, event | category | flops | bytes accessed | tf_op | source)
XLA Modules:
  0.0 729.8 jit_solution(5748484860902074060)
XLA Ops:
  6.5 0.7 fusion.37
  7.3 4.3 collective-permute-start.1
  11.6 1.3 collective-permute-start
  12.9 0.7 constant_dynamic-update-slice_fusion.1
  13.7 2.5 collective-permute-done
  16.2 3.8 collective-permute-start.2
  20.1 7.8 %collective-permute-start.3 = (f32[4,1,512]{2,1,0:T(1,128)S(1)}, f32[4,1,512]{2,1,0:T(1,128)S(1)}, u32[]{:S(2)}, u32[]{:S(2)}) collective-permute-start(f32[4,1,512]{2,1,0:T(1,128)S(1)} %get-tuple-element.9), channel_id=1, source_target_pairs={{0,1},{1,2},{2,3},{3,4},{4,5},{5,6},{6,7},{7,8},{8,9},{9,10},{10,1... | collective-permute-start | bytes 24584 | tf_op jit(solution)/shard_map/ppermute | solution.py:16
  27.9 0.8 dynamic-slice_convert_fusion.1
  28.7 0.1 select_maximum_fusion
  28.8 0.9 fusion.29
  29.7 2.7 multiply_convert_fusion
  32.5 0.1 copy-done
  32.6 1.7 convolution_bitcast_fusion.2
  34.3 0.2 mul.100
  34.5 0.8 bitcast_multiply_fusion
  35.3 0.2 mul.96
  35.6 0.9 fusion.35
  36.6 0.1 broadcast_bitcast_fusion
  36.7 175.1 %all-reduce.3.cloned.1.call-done = f32[3,128,128]{2,1,0:T(8,128)} async-done(((f32[3,128,128]{2,1,0:T(8,128)}), f32[3,128,128]{2,1,0:T(8,128)}) %all-reduce.3.cloned.1.call-update) | async-done | bytes 196624 | tf_op jit(solution)/shard_map/psum | solution.py:40
  211.8 1.2 convolution_bitcast_fusion.1
  213.1 0.1 copy.18
  213.2 82.5 %all-gather.6.cloned.1.call-done = bf16[384,6144]{1,0:T(8,128)(2,1)} async-done(((bf16[384,384]{1,0:T(8,128)(2,1)}), bf16[384,6144]{1,0:T(8,128)(2,1)}) %all-gather.6.cloned.1.call-update) | async-done | bytes 4718608 | tf_op jit(solution)/shard_map/all_gather | solution.py:71
  295.7 203.1 %all-gather.4.cloned.1.call-done = bf16[2,6144,384]{2,1,0:T(8,128)(2,1)} async-done(((bf16[2,384,384]{2,1,0:T(8,128)(2,1)}), bf16[2,6144,384]{2,1,0:T(8,128)(2,1)}) %all-gather.4.cloned.1.call-update) | async-done | bytes 9437200 | tf_op jit(solution)/shard_map/all_gather | solution.py:68
  498.8 10.2 %fusion.38 = (bf16[2,384,384]{2,1,0:T(8,128)(2,1)}, f32[2,384,384]{2,1,0:T(8,128)}) fusion(f32[2,384,384]{2,1,0:T(8,128)S(1)} %bitcast.74, bf16[2,6144,384]{2,1,0:T(8,128)(2,1)} %all-gather.4.cloned.1.call-done, bf16[384,6144]{1,0:T(8,128)(2,1)} %all-gather.6.cloned.1.call-done), kind=kOutput, calls=%fused_computation.61 | convolution fusion | flops 3624468480 | bytes 17104896 | tf_op jit(solution)/shard_map/rk,skc->src/dot_general | solution.py:69
  509.0 0.2 mul.119
  509.2 0.8 copy-done.1
  510.0 0.3 convolution_bitcast_fusion
  510.3 0.1 copy.22
  510.4 203.2 %all-gather.8.cloned.1.call-done = bf16[2,6144,384]{2,1,0:T(8,128)(2,1)} async-done(((bf16[2,384,384]{2,1,0:T(8,128)(2,1)}), bf16[2,6144,384]{2,1,0:T(8,128)(2,1)}) %all-gather.8.cloned.1.call-update) | async-done | bytes 9437200 | tf_op jit(solution)/shard_map/all_gather | solution.py:68
  713.6 8.5 %fusion.13 = f32[2,384,384]{2,1,0:T(8,128)S(1)} fusion(f32[2,384,384]{2,1,0:T(8,128)S(1)} %bitcast.75, bf16[2,6144,384]{2,1,0:T(8,128)(2,1)} %all-gather.8.cloned.1.call-done, bf16[384,6144]{1,0:T(8,128)(2,1)} %all-gather.6.cloned.1.call-done), kind=kOutput, calls=%fused_computation.10 | convolution fusion | flops 3624173568 | bytes 16515072 | tf_op jit(solution)/shard_map/rk,skc->src/dot_general | solution.py:69
  722.1 0.3 fusion.19
  722.4 0.9 fusion.16
  (27 shorter events, 0.4 us)
Async XLA Ops:
  6.5 205.3 %all-reduce.3.cloned.1.call-start = ((), (), s32[]{:S(2)}) async-start(), calls=%async_computation.2 | async-start | bytes 393216 | tf_op jit(solution)/shard_map/psum | solution.py:40
  7.3 5.7 collective-permute-start.1
  11.6 4.6 collective-permute-start
  16.2 12.5 %collective-permute-start.2 = (f32[4,1,512]{2,1,0:T(1,128)S(1)}, f32[4,1,512]{2,1,0:T(1,128)S(1)}, u32[]{:S(2)}, u32[]{:S(2)}) collective-permute-start(f32[4,1,512]{2,1,0:T(1,128)S(1)} %get-tuple-element.10), channel_id=1, source_target_pairs={{1,0},{2,1},{3,2},{4,3},{5,4},{6,5},{7,6},{8,7},{9,8},{10,9},{11,1... | collective-permute-start | bytes 24584 | tf_op jit(solution)/shard_map/ppermute | solution.py:19
  20.1 8.6 %collective-permute-start.3 = (f32[4,1,512]{2,1,0:T(1,128)S(1)}, f32[4,1,512]{2,1,0:T(1,128)S(1)}, u32[]{:S(2)}, u32[]{:S(2)}) collective-permute-start(f32[4,1,512]{2,1,0:T(1,128)S(1)} %get-tuple-element.9), channel_id=1, source_target_pairs={{0,1},{1,2},{2,3},{3,4},{4,5},{5,6},{6,7},{7,8},{8,9},{9,10},{10,1... | collective-permute-start | bytes 24584 | tf_op jit(solution)/shard_map/ppermute | solution.py:16
  29.7 2.8 copy-start
  32.6 1.9 copy-start.5
  32.6 3.0 copy-start.2
  34.2 261.5 %all-gather.6.cloned.1.call-start = ((), (), s32[]{:S(2)}) async-start(), calls=%async_computation.1 | async-start | bytes 5013504 | tf_op jit(solution)/shard_map/all_gather | solution.py:71
  35.3 463.5 %all-gather.4.cloned.1.call-start = ((), (), s32[]{:S(2)}) async-start(), calls=%async_computation | async-start | bytes 10027008 | tf_op jit(solution)/shard_map/all_gather | solution.py:68
  36.6 677.0 %all-gather.8.cloned.1.call-start = ((), (), s32[]{:S(2)}) async-start(), calls=%async_computation.3 | async-start | bytes 10027008 | tf_op jit(solution)/shard_map/all_gather | solution.py:68
  498.8 10.4 %copy-start.4 = (f32[3,128,128]{2,1,0:T(8,128)S(1)}, f32[3,128,128]{2,1,0:T(8,128)}, u32[]{:S(2)}) copy-start(f32[3,128,128]{2,1,0:T(8,128)} %all-reduce.3.cloned.1.call-done) | copy-start | bytes 589828
  508.9 1.1 copy-start.1
  713.6 8.5 %copy-start.3 = (f32[2,384,384]{2,1,0:T(8,128)S(1)}, f32[2,384,384]{2,1,0:T(8,128)}, u32[]{:S(2)}) copy-start(f32[2,384,384]{2,1,0:T(8,128)} %get-tuple-element.16) | copy-start | bytes 3538948
Sparse Core Ops, SparseCore 0:
  34.4 177.4 all-reduce.2
  214.4 81.2 all-gather.5
  297.5 201.2 all-gather.3
  509.1 204.4 all-gather.7
where the time goes:
time: 730 us
  waiting for transfers between devices  667 us (91%)
  matrix products  21.9 us (3%)
  starting transfers between devices  17.4 us (2%)
  between operations  13.3 us (2%)
  other arithmetic  7.46 us (1%)
    all_gather x2, waiting for transfers between devices, apply(): column_whole = lax.all_gather(operand, 'row', axis=1, tiled=True)  406 us
    psum x1, waiting for transfers between devices, shards(): summed = lax.psum(partial_blocks, 'col')  175 us
    all_gather x1, waiting for transfers between devices, apply(): lax.all_gather(masked_h, 'col', axis=1, tiled=True)  82.5 us
    dot_general x2, matrix products, apply(): jnp.einsum('rk,skc->src', lax.all_gather(masked_h, 'col', axis=1, tiled=T...  18.7 us
  transfers between devices with their start and end apart: 8, of which 5 were waited for; matrix products, arithmetic and copies ran while one was open for 1% of the time, Pallas kernels for 0%

commit v1 on v0

--- a/solution.py
+++ b/solution.py
@@ -2,6 +2,7 @@
 import jax.numpy as jnp
 from jax import lax
 from jax.sharding import PartitionSpec as P
+from jax.lax import all_to_all, psum
 
 BLK = 128
 KAPPA = 0.4
@@ -68,7 +69,15 @@
         column_whole = lax.all_gather(operand, "row", axis=1, tiled=True)
         remote = jnp.einsum(
             "rk,skc->src",
-            lax.all_gather(masked_h, "col", axis=1, tiled=True),
+            jnp.concatenate(
+                all_to_all(
+                    jnp.stack([masked_h for _ in range(psum(1, "col"))], axis=0),
+                    "col",
+                    split_axis=0,
+                    concat_axis=0,
+                ),
+                axis=1,
+            ),
             column_whole,
             preferred_element_type=jnp.float32,
         )

time: 730 us -> 689 us (0.944)
  waiting for transfers between devices: 667 us -> 596 us
  local copies, waits for them, and re-layouts: 3.23 us -> 20.9 us
  starting transfers between devices: 17.4 us -> 27.8 us
    psum x1, waiting for transfers between devices: 175 us -> 389 us  [shards(): summed = lax.psum(partial_blocks, 'col')]
    all_gather x2, waiting for transfers between devices: 406 us -> 204 us  [apply(): column_whole = lax.all_gather(operand, 'row', axis=1, tiled=True)]
    all_gather x1 -> x0, waiting for transfers between devices: 82.5 us -> none  [apply(): lax.all_gather(masked_h, 'col', axis=1, tiled=True)]
    reshape x0 -> x2, local copies, waits for them, and re-layouts: none -> 15 us  [apply(): jnp.concatenate(all_to_all(jnp.stack([masked_h for _ in range(psum(1, 'co...]
    all_to_all x0 -> x1, starting transfers between devices: none -> 10.2 us  [apply(): all_to_all(jnp.stack([masked_h for _ in range(psum(1, 'col'))], axis=0),...]
  transfers between devices with their start and end apart: 8 -> 8, of which waited for: 5 -> 3; matrix products, arithmetic and copies ran while one was open for 1% -> 3% of each run, Pallas kernels for 0% -> 0%
where the time goes in v1:
time: 689 us; the launch traced here: 688 us
  waiting for transfers between devices  596 us (87%)
  starting transfers between devices  27.8 us (4%)
  matrix products  21.9 us (3%)
  local copies, waits for them, and re-layouts  20.9 us (3%)
  between operations  15.1 us (2%)
    psum x1, waiting for transfers between devices, shards(): summed = lax.psum(partial_blocks, 'col')  389 us
    all_gather x2, waiting for transfers between devices, apply(): column_whole = lax.all_gather(operand, 'row', axis=1, tiled=True)  204 us
    dot_general x2, matrix products, apply(): jnp.einsum('rk,skc->src', jnp.concatenate(all_to_all(jnp.stack([masked_h...  18.7 us
    reshape x2, local copies, waits for them, and re-layouts, apply(): jnp.concatenate(all_to_all(jnp.stack([masked_h for _ in range(psum(1, 'co...  15 us
  transfers between devices with their start and end apart: 8, of which 3 were waited for; matrix products, arithmetic and copies ran while one was open for 3% of the time, Pallas kernels for 0%

profile of v1, /device:TPU:1, one launch (start us, length us, event | category | flops | bytes accessed | tf_op | source)
XLA Modules:
  0.0 688.0 jit_solution(5584592579149452182)
XLA Ops:
  7.4 0.7 fusion.23
  8.1 4.3 collective-permute-start.1
  12.4 1.3 collective-permute-start
  13.8 0.7 constant_dynamic-update-slice_fusion.1
  14.5 2.5 collective-permute-done
  17.1 3.8 collective-permute-start.2
  20.9 7.8 %collective-permute-start.3 = (f32[4,1,512]{2,1,0:T(1,128)S(1)}, f32[4,1,512]{2,1,0:T(1,128)S(1)}, u32[]{:S(2)}, u32[]{:S(2)}) collective-permute-start(f32[4,1,512]{2,1,0:T(1,128)S(1)} %get-tuple-element.9), channel_id=1, source_target_pairs={{0,1},{1,2},{2,3},{3,4},{4,5},{5,6},{6,7},{7,8},{8,9},{9,10},{10,1... | collective-permute-start | bytes 24584 | tf_op jit(solution)/shard_map/ppermute | solution.py:17
  28.7 0.8 dynamic-slice_convert_fusion.1
  29.5 0.2 mul.97
  29.8 0.1 select_maximum_fusion
  29.9 0.9 fusion.15
  30.8 2.7 multiply_convert_fusion
  33.5 0.1 copy-done
  33.6 1.7 convolution_bitcast_fusion.4
  35.4 0.9 fusion.21
  36.4 0.2 mul.101
  36.6 2.7 stack.4
  39.3 10.2 %all-to-all-start = ((bf16[16,384,384]{2,1,0:T(8,128)(2,1)}), bf16[16,384,384]{2,1,0:T(8,128)(2,1)}, u32[]{:S(2)}, u32[]{:S(2)}) async-start(bf16[16,384,384]{2,1,0:T(8,128)(2,1)} %stack.4), calls=%async_computation | async-start | bytes 9437184 | tf_op jit(solution)/shard_map/all_to_all | solution.py:73
  49.6 0.2 all-gather.5.cloned.1.call-start
  49.9 389.2 %all-reduce.3.cloned.1.call-done = f32[3,128,128]{2,1,0:T(8,128)} async-done(((f32[3,128,128]{2,1,0:T(8,128)}), f32[3,128,128]{2,1,0:T(8,128)}) %all-reduce.3.cloned.1.call-update) | async-done | bytes 196624 | tf_op jit(solution)/shard_map/psum | solution.py:41
  439.1 1.2 convolution_bitcast_fusion.2
  440.4 7.2 %copy.23 = bf16[384,16,384]{2,1,0:T(8,128)(2,1)} copy(bf16[384,16,384]{2,0,1:T(8,128)(2,1)} %bitcast) | data formatting | bytes 9437184 | tf_op jit(solution)/shard_map/reshape | solution.py:72
  447.7 7.7 %reshape.59 = bf16[384,6144,1]{1,0,2:T(8,128)(2,1)} reshape(bf16[384,16,384]{2,1,0:T(8,128)(2,1)} %copy.23) | data formatting | bytes 9437184 | tf_op jit(solution)/shard_map/reshape | solution.py:72
  455.4 10.2 %fusion.24 = (bf16[2,384,384]{2,1,0:T(8,128)(2,1)}, f32[2,384,384]{2,1,0:T(8,128)}) fusion(f32[2,384,384]{2,1,0:T(8,128)S(1)} %bitcast.62, bf16[384,6144,1]{1,0,2:T(8,128)(2,1)} %reshape.59, bf16[2,6144,384]{2,1,0:T(8,128)(2,1)} %all-gather.3.cloned.1.call-done), kind=kOutput, calls=%fused_computation.57 | convolution fusion | flops 3624468480 | bytes 17104896 | tf_op jit(solution)/shard_map/rk,skc->src/dot_general | solution.py:70
  465.6 0.2 mul.120
  465.8 0.8 copy-done.1
  466.6 0.3 convolution_bitcast_fusion
  466.9 0.1 copy.29
  467.0 203.9 %all-gather.5.cloned.1.call-done = bf16[2,6144,384]{2,1,0:T(8,128)(2,1)} async-done(((bf16[2,384,384]{2,1,0:T(8,128)(2,1)}), bf16[2,6144,384]{2,1,0:T(8,128)(2,1)}) %all-gather.5.cloned.1.call-update) | async-done | bytes 9437200 | tf_op jit(solution)/shard_map/all_gather | solution.py:69
  670.9 8.5 %fusion.1 = f32[2,384,384]{2,1,0:T(8,128)S(1)} fusion(f32[2,384,384]{2,1,0:T(8,128)S(1)} %bitcast.63, bf16[384,6144,1]{1,0,2:T(8,128)(2,1)} %reshape.59, bf16[2,6144,384]{2,1,0:T(8,128)(2,1)} %all-gather.5.cloned.1.call-done), kind=kOutput, calls=%fused_computation.6 | convolution fusion | flops 3624173568 | bytes 16515072 | tf_op jit(solution)/shard_map/rk,skc->src/dot_general | solution.py:70
  679.4 0.3 fusion.5
  679.7 0.9 fusion.2
  (29 shorter events, 0.5 us)
Async XLA Ops:
  7.4 431.7 %all-reduce.3.cloned.1.call-start = ((), (), s32[]{:S(2)}) async-start(), calls=%async_computation.2 | async-start | bytes 393216 | tf_op jit(solution)/shard_map/psum | solution.py:41
  8.1 5.7 collective-permute-start.1
  12.4 4.6 collective-permute-start
  17.1 12.7 %collective-permute-start.2 = (f32[4,1,512]{2,1,0:T(1,128)S(1)}, f32[4,1,512]{2,1,0:T(1,128)S(1)}, u32[]{:S(2)}, u32[]{:S(2)}) collective-permute-start(f32[4,1,512]{2,1,0:T(1,128)S(1)} %get-tuple-element.10), channel_id=1, source_target_pairs={{1,0},{2,1},{3,2},{4,3},{5,4},{6,5},{7,6},{8,7},{9,8},{10,9},{11,1... | collective-permute-start | bytes 24584 | tf_op jit(solution)/shard_map/ppermute | solution.py:20
  20.9 8.9 %collective-permute-start.3 = (f32[4,1,512]{2,1,0:T(1,128)S(1)}, f32[4,1,512]{2,1,0:T(1,128)S(1)}, u32[]{:S(2)}, u32[]{:S(2)}) collective-permute-start(f32[4,1,512]{2,1,0:T(1,128)S(1)} %get-tuple-element.9), channel_id=1, source_target_pairs={{0,1},{1,2},{2,3},{3,4},{4,5},{5,6},{6,7},{7,8},{8,9},{9,10},{10,1... | collective-permute-start | bytes 24584 | tf_op jit(solution)/shard_map/ppermute | solution.py:17
  30.8 2.8 copy-start
  33.6 1.7 copy-start.2
  35.3 1.2 copy-start.5
  35.3 420.1 %all-gather.3.cloned.1.call-start = ((), (), s32[]{:S(2)}) async-start(), calls=%async_computation.1 | async-start | bytes 10027008 | tf_op jit(solution)/shard_map/all_gather | solution.py:69
  39.3 401.1 %all-to-all-start = ((bf16[16,384,384]{2,1,0:T(8,128)(2,1)}), bf16[16,384,384]{2,1,0:T(8,128)(2,1)}, u32[]{:S(2)}, u32[]{:S(2)}) async-start(bf16[16,384,384]{2,1,0:T(8,128)(2,1)} %stack.4), calls=%async_computation | async-start | bytes 9437184 | tf_op jit(solution)/shard_map/all_to_all | solution.py:73
  49.6 621.3 %all-gather.5.cloned.1.call-start = ((), (), s32[]{:S(2)}) async-start(), calls=%async_computation.3 | async-start | bytes 10027008 | tf_op jit(solution)/shard_map/all_gather | solution.py:69
  455.4 10.4 %copy-start.4 = (f32[3,128,128]{2,1,0:T(8,128)S(1)}, f32[3,128,128]{2,1,0:T(8,128)}, u32[]{:S(2)}) copy-start(f32[3,128,128]{2,1,0:T(8,128)} %all-reduce.3.cloned.1.call-done) | copy-start | bytes 589828
  465.5 1.1 copy-start.1
  670.9 8.5 %copy-start.3 = (f32[2,384,384]{2,1,0:T(8,128)S(1)}, f32[2,384,384]{2,1,0:T(8,128)}, u32[]{:S(2)}) copy-start(f32[2,384,384]{2,1,0:T(8,128)} %get-tuple-element.16) | copy-start | bytes 3538948
Sparse Core Ops, SparseCore 0:
  35.4 403.6 all-reduce.2
Sparse Core Ops, SparseCore 1:
  37.6 312.0 all-gather.2
  465.7 205.2 all-gather.4
